TPU v7x, 256 devices: a whole 4x4x8 slice. The times are simulated.
256 devices in a mesh: replica: 16 (over z, core), mp: 16 (over y, x).
Axes of the slice: x: 4, y: 4, z: 8, core: 2. Of those that a mesh axis runs over, the one named last changes fastest.
Arguments:
- gradients: bfloat16 [16, 8, 768, 3072], P('replica', None, 'mp'), may hold values from -6 to 6
- feedback: bfloat16 [16, 8, 768, 3072], P('replica', None, 'mp'), may hold values from -4 to 4
- right_init: bfloat16 [8, 3072, 32], replicated, may hold values from -0.109375 to 0.109375
- gram_root: float32 [8, 32, 32], replicated, as said below
- owners: int32 [8], replicated, may hold values from 0 to 15, as said below
- momentum: float32 [16, 1, 768, 3072], P('mp', None, 'replica'), may hold values from -4 to 4
- master_weights: float32 [16, 1, 768, 3072], P('mp', None, 'replica'), may hold values from -1.5 to 1.5
- vector_grads: float32 [16, 10752], P('replica', 'mp'), may hold values from -6 to 6
- vector_momentum: float32 [10752], P('mp'), may hold values from -6 to 6
- vector_params: float32 [10752], P('mp'), may hold values from -6 to 6
Outputs:
- new_feedback: bfloat16 [16, 8, 768, 3072], P('replica', None, 'mp')
- new_momentum: float32 [16, 1, 768, 3072], P('mp', None, 'replica')
- new_master: float32 [16, 1, 768, 3072], P('mp', None, 'replica')
- new_weights: bfloat16 [8, 768, 3072], P(None, 'replica')
- new_vector_momentum: float32 [10752], P('mp')
- new_vector_params: float32 [10752], P('mp')
Inputs may be any that keep to these rules, and one draw needn't show every extreme that they name: `owners`: every matrix has one owner; no owner holds more than 1 of the 8 matrices, and one owner holds exactly 1. `gram_root`: each matrix is the identity plus off-diagonal terms, times a positive scale.
All inputs are finite; a program needn't handle non-finite values.
Results may differ from a plain program's by a relative error of at most 0.007.
Values may be sent and summed in bfloat16 or wider, within the bound.
A program may use at most 192 MiB of HBM per device.

v0:
```python
import jax
import jax.numpy as jnp
from jax import lax
from jax.sharding import PartitionSpec as P


def per_device(
    gradients,
    feedback,
    right_init,
    gram_root,
    owners,
    momentum,
    master_weights,
    vector_grads,
    vector_momentum,
    vector_params,
):
    highest = lax.Precision.HIGHEST
    compensated = (gradients[0].astype(jnp.float32) + feedback[0].astype(jnp.float32)).astype(
        jnp.bfloat16
    )
    owner_count = lax.axis_size("mp")
    capacity = momentum.shape[1]
    matrices = owners.shape[0]
    replica_rows = momentum.shape[2]
    mp_index = lax.axis_index("mp")
    replica_index = lax.axis_index("replica")
    same_owner = owners[:, None] == owners[None, :]
    earlier = jnp.arange(matrices)[:, None] < jnp.arange(matrices)[None, :]
    ranks = jnp.sum((same_owner & earlier).astype(jnp.int32), axis=0)
    slots = owners * capacity + ranks
    mine = slots[None, :] == (mp_index * capacity + jnp.arange(capacity))[:, None]
    has = jnp.any(mine, axis=1)
    chosen = jnp.argmax(mine, axis=1)
    left_terms = jnp.einsum(
        "kmn,knr->kmr", compensated, right_init, preferred_element_type=jnp.float32
    )
    left_sum = lax.psum(left_terms, "replica")
    left_rows = jnp.einsum("kmr,krs->kms", left_sum, gram_root, precision=highest).astype(
        jnp.bfloat16
    )
    right_terms = jnp.einsum(
        "kmn,kms->kns", compensated, left_rows, preferred_element_type=jnp.float32
    )
    right_part = lax.psum_scatter(right_terms.reshape(-1), "mp", scatter_dimension=0, tiled=True)
    right_part = lax.psum(right_part, "replica")
    right_new = lax.all_gather(right_part.astype(jnp.bfloat16), "mp", axis=0, tiled=True).reshape(
        right_terms.shape
    )
    left_all = lax.all_gather(left_rows, "mp", axis=1, tiled=True)
    approx_rows = jnp.einsum(
        "kms,kns->kmn", left_rows, right_new, preferred_element_type=jnp.float32
    )
    new_feedback = (compensated.astype(jnp.float32) - approx_rows).astype(jnp.bfloat16)
    scale = has.astype(jnp.float32)[:, None, None]
    left_chosen = (
        lax.dynamic_slice_in_dim(
            left_all[chosen], replica_index * replica_rows, replica_rows, 1
        ).astype(jnp.float32)
        * scale
    )
    right_chosen = right_new[chosen].astype(jnp.float32) * scale
    approx_slots = jnp.einsum("cmr,cnr->cmn", left_chosen, right_chosen, precision=highest)
    new_momentum = 0.9 * momentum[0] + approx_slots
    new_master = master_weights[0] - 0.1 * new_momentum
    master_narrow = new_master.astype(jnp.bfloat16)
    weight_slots = lax.all_gather(master_narrow, "mp", axis=0, tiled=True)
    new_weights = jnp.take(weight_slots, slots, axis=0)
    vector_total = lax.psum(vector_grads[0], "replica")
    new_vector_momentum = 0.9 * vector_momentum + vector_total
    new_vector_params = vector_params - 0.1 * new_vector_momentum
    return (
        new_feedback[None],
        new_momentum[None],
        new_master[None],
        new_weights,
        new_vector_momentum,
        new_vector_params,
    )


def solution(mesh):
    return jax.shard_map(
        per_device,
        mesh=mesh,
        in_specs=(
            P("replica", None, "mp", None),
            P("replica", None, "mp", None),
            P(),
            P(),
            P(),
            P("mp", None, "replica", None),
            P("mp", None, "replica", None),
            P("replica", "mp"),
            P("mp"),
            P("mp"),
        ),
        out_specs=(
            P("replica", None, "mp", None),
            P("mp", None, "replica", None),
            P("mp", None, "replica", None),
            P(None, "replica", None),
            P("mp"),
            P("mp"),
        ),
        check_vma=False,
    )
```

profile of v0, /device:TPU:1, one launch (start us, length us, event | category | flops | bytes accessed | tf_op | source)
XLA Modules:
  0.0 369.8 jit_solution(15668243150370292519)
XLA Ops:
  7.2 1.3 copy-done
  8.6 3.1 fusion.14
  11.7 49.7 %psum.21 = f32[8,48,32]{1,2,0:T(8,128)S(1)} all-reduce(f32[8,48,32]{1,2,0:T(8,128)S(1)} %fusion.14), channel_id=1, replica_groups=mesh['replica'=16,'mp'=16] {'replica'}, use_global_device_ids=true, to_apply=%region_0.0 | all-reduce | flops 12288 | bytes 98304 | tf_op jit(solution)/shard_map/psum | solution.py:39
  61.4 0.4 convolution_convert_fusion
  61.8 9.0 %fusion.12 = f32[8,3072,32]{2,1,0:T(8,128)} fusion(bf16[8,48,32]{1,2,0:T(8,128)(2,1)S(1)} %convolution_convert_fusion, bf16[1,8,48,3072]{3,2,1,0:T(8,128)(2,1)} %param.11, bf16[1,8,48,3072]{3,2,1,0:T(8,128)(2,1)} %param.10), kind=kOutput, calls=%fused_computation.29 | convolution fusion | flops 80216064 | bytes 7888896 | tf_op jit(solution)/shard_map/kmn,kms->kns/dot_general | solution.py:43
  70.8 9.4 %reshape.76 = f32[786432]{0:T(1024)} reshape(f32[8,3072,32]{2,1,0:T(8,128)} %fusion.12) | data formatting | bytes 6291456 | tf_op jit(solution)/shard_map/reshape | solution.py:46
  80.3 0.6 copy-done.9
  80.9 0.6 dynamic-slice.8
  82.1 104.3 %all-reduce.5.cloned.1.call-done = f32[786432]{0:T(1024)} async-done(((f32[786432]{0:T(1024)}), f32[786432]{0:T(1024)}) %all-reduce.5.cloned.1.call-update) | async-done | bytes 3145744
  186.4 0.9 dynamic-slice.9
  187.3 48.4 %all-reduce.6 = (bf16[49152]{0:T(1024)(128)(2,1)}, f32[672]{0:T(1024)S(1)}) all-reduce(f32[49152]{0:T(1024)S(1)} %dynamic-slice.9, f32[672]{0:T(1024)S(1)} %reduce.20), channel_id=1, replica_groups=mesh['replica'=16,'mp'=16] {'replica'}, use_global_device_ids=true, to_apply=%region_2.0 | all-reduce | flops 49824 | bytes 300288 | tf_op jit(solution)/shard_map/psum | solution.py:47
  235.8 0.1 copy.27
  236.0 0.7 bitcast_reduce_fusion
  238.0 0.6 compare_and_fusion
  239.9 21.6 %all_gather.10 = bf16[8,768,32]{2,0,1:T(8,128)(2,1)S(1)} all-gather(bf16[8,48,32]{2,0,1:T(8,128)(2,1)S(1)} %copy.27), channel_id=1, replica_groups=mesh['replica'=16,'mp'=16] {'mp'}, dimensions={1}, use_global_device_ids=true | all-gather | bytes 417792 | tf_op jit(solution)/shard_map/all_gather | solution.py:51
  261.5 22.4 %all-gather.4.cloned.1.call-done = bf16[786432]{0:T(1024)(128)(2,1)} async-done(((bf16[49152]{0:T(1024)(128)(2,1)}), bf16[786432]{0:T(1024)(128)(2,1)}) %all-gather.4.cloned.1.call-update) | async-done | bytes 1572880 | tf_op jit(solution)/shard_map/all_gather | solution.py:48
  283.9 7.8 %reshape.77 = bf16[8,3072,32]{2,1,0:T(8,128)(2,1)} reshape(bf16[786432]{0:T(1024)(128)(2,1)} %all-gather.4.cloned.1.call-done) | data formatting | bytes 3145728 | tf_op jit(solution)/shard_map/reshape | solution.py:48
  291.8 3.0 convolution_add_fusion
  294.8 1.1 fusion.7
  295.9 0.6 multiply_subtract_fusion
  296.5 7.9 %fusion = bf16[1,8,48,3072]{3,2,1,0:T(8,128)(2,1)} fusion(bf16[8,48,32]{1,2,0:T(8,128)(2,1)S(1)} %convolution_convert_fusion, bf16[8,3072,32]{2,1,0:T(8,128)(2,1)} %reshape.77, bf16[1,8,48,3072]{3,2,1,0:T(8,128)(2,1)} %param.11, bf16[1,8,48,3072]{3,2,1,0:T(8,128)(2,1)} %param.10), kind=kOutput, calls=%fused_computation.3 | convolution fusion | flops 83755008 | bytes 8675328 | tf_op jit(solution)/shard_map/kms,kns->kmn/dot_general | solution.py:52
  304.4 51.0 %all-gather.6.cloned.1.call-done = bf16[768,3072]{1,0:T(8,128)(2,1)} async-done(((bf16[48,3072]{1,0:T(8,128)(2,1)}), bf16[768,3072]{1,0:T(8,128)(2,1)}) %all-gather.6.cloned.1.call-update) | async-done | bytes 4718608 | tf_op jit(solution)/shard_map/all_gather | solution.py:68
  355.4 4.4 %gather_fusion = bf16[8,48,3072]{2,1,0:T(8,128)(2,1)} fusion(bf16[16,48,3072]{2,1,0:T(8,128)(2,1)} %bitcast.36, s32[1024]{0:T(1024)S(1)} %pad_clamp_fusion), kind=kCustom, calls=%fused_computation | custom fusion | bytes 4718624 | tf_op jit(solution)/shard_map/jit(_take)/gather | solution.py:69
  359.9 3.4 broadcast_select_fusion
  (28 shorter events, 0.4 us)
Async XLA Ops:
  7.2 1.4 copy-start
  7.2 54.2 %copy-start.4 = (f32[8,32,32]{2,1,0:T(8,128)S(1)}, f32[8,32,32]{2,1,0:T(8,128)}, u32[]{:S(2)}) copy-start(f32[8,32,32]{2,1,0:T(8,128)} %param.13) | copy-start | bytes 98308
  7.2 179.2 %all-reduce.5.cloned.1.call-start = ((), (), s32[]{:S(2)}) async-start(), calls=%async_computation.2 | async-start | bytes 6291456
  80.2 0.7 copy-start.9
  80.2 1.9 copy-start.7
  80.2 155.7 %copy-start.8 = (s32[8]{0:T(128)S(1)}, s32[8]{0:T(128)}, u32[]{:S(2)}) copy-start(s32[8]{0:T(128)} %param.14) | copy-start | bytes 100
  80.2 203.7 %all-gather.4.cloned.1.call-start = ((), (), s32[]{:S(2)}) async-start(), calls=%async_computation | async-start | bytes 1671168 | tf_op jit(solution)/shard_map/all_gather | solution.py:48
  235.7 119.7 %all-gather.6.cloned.1.call-start = ((), (), s32[]{:S(2)}) async-start(), calls=%async_computation.1 | async-start | bytes 5013504 | tf_op jit(solution)/shard_map/all_gather | solution.py:68
  261.5 30.2 %copy-start.2 = (f32[1,1,48,3072]{3,2,1,0:T(8,128)S(1)}, f32[1,1,48,3072]{3,2,1,0:T(8,128)}, u32[]{:S(2)}) copy-start(f32[1,1,48,3072]{3,2,1,0:T(8,128)} %param.15) | copy-start | bytes 1769476
  291.7 3.0 copy-start.3
  291.8 4.1 %copy-start.5 = (f32[672]{0:T(1024)S(1)}, f32[672]{0:T(1024)}, u32[]{:S(2)}) copy-start(f32[672]{0:T(1024)} %param.19) | copy-start | bytes 8068
  291.8 4.2 %copy-start.6 = (f32[672]{0:T(1024)S(1)}, f32[672]{0:T(1024)}, u32[]{:S(2)}) copy-start(f32[672]{0:T(1024)} %param.18) | copy-start | bytes 8068
  294.8 9.7 %copy-start.1 = (f32[48,3072]{1,0:T(8,128)}, f32[48,3072]{1,0:T(8,128)S(1)}, u32[]{:S(2)}) copy-start(f32[48,3072]{1,0:T(8,128)S(1)} %convolution_add_fusion) | copy-start | bytes 1769476
Sparse Core Ops, SparseCore 0:
  80.3 106.0 all-reduce.4
  235.8 48.0 all-gather.3
  296.0 59.3 all-gather.5
where the time goes:
time: 370 us
  waiting for transfers between devices  178 us (48%)
  blocking collectives  120 us (32%)
  local copies, waits for them, and re-layouts  25.3 us (7%)
  matrix products  23.4 us (6%)
  between operations  17.2 us (5%)
  other arithmetic  6.49 us (2%)
    unnamed x4, waiting for transfers between devices  104 us
    all_gather x1, waiting for transfers between devices, per_device(): weight_slots = lax.all_gather(master_narrow, 'mp', axis=0, tiled=True)  51 us
    psum x1, blocking collectives, per_device(): left_sum = lax.psum(left_terms, 'replica')  49.7 us
    psum x1, blocking collectives, per_device(): right_part = lax.psum(right_part, 'replica')  48.4 us
    all_gather x1, waiting for transfers between devices, per_device(): lax.all_gather(right_part.astype(jnp.bfloat16), 'mp', axis=0, tiled=True)  22.4 us
    all_gather x1, blocking collectives, per_device(): left_all = lax.all_gather(left_rows, 'mp', axis=1, tiled=True)  21.6 us
    reshape x1, local copies, waits for them, and re-layouts, per_device(): right_terms.reshape(-1)  9.41 us
    dot_general x1, matrix products, per_device(): jnp.einsum('kmn,kms->kns', compensated, left_rows, preferred_element_type...  8.99 us
  transfers between devices with their start and end apart: 3, of which 3 were waited for; matrix products, arithmetic and copies ran while one was open for 3% of the time, Pallas kernels for 0%

commit v1 on v0

--- a/solution.py
+++ b/solution.py
@@ -44,7 +44,7 @@
         "kmn,kms->kns", compensated, left_rows, preferred_element_type=jnp.float32
     )
     right_part = lax.psum_scatter(right_terms.reshape(-1), "mp", scatter_dimension=0, tiled=True)
-    right_part = lax.psum(right_part, "replica")
+    right_part = jnp.sum(lax.all_gather(right_part, "replica"), axis=0)
     right_new = lax.all_gather(right_part.astype(jnp.bfloat16), "mp", axis=0, tiled=True).reshape(
         right_terms.shape
     )

time: 370 us -> 370 us (level)
  blocking collectives: 120 us -> 73.1 us
  waiting for transfers between devices: 178 us -> 217 us
  other arithmetic: 6.49 us -> 10.3 us
    psum x1 -> x0, blocking collectives: 48.4 us -> none  [per_device(): right_part = lax.psum(right_part, 'replica')]
    all_gather x0 -> x1, waiting for transfers between devices: none -> 41.7 us  [per_device(): right_part = jnp.sum(lax.all_gather(right_part, 'replica'), axis=0)]
    unnamed x4 -> x5, waiting for transfers between devices: 104 us -> 104 us
  transfers between devices with their start and end apart: 3 -> 4, of which waited for: 3 -> 4; matrix products, arithmetic and copies ran while one was open for 3% -> 3% of each run, Pallas kernels for 0% -> 0%
where the time goes in v1:
time: 370 us
  waiting for transfers between devices  217 us (59%)
  blocking collectives  73.1 us (20%)
  local copies, waits for them, and re-layouts  28.6 us (8%)
  matrix products  23.4 us (6%)
  between operations  17.2 us (5%)
  other arithmetic  10.3 us (3%)
    unnamed x5, waiting for transfers between devices  104 us
    all_gather x1, waiting for transfers between devices, per_device(): weight_slots = lax.all_gather(master_narrow, 'mp', axis=0, tiled=True)  51 us
    psum x1, blocking collectives, per_device(): left_sum = lax.psum(left_terms, 'replica')  50.5 us
    all_gather x1, waiting for transfers between devices, per_device(): right_part = jnp.sum(lax.all_gather(right_part, 'replica'), axis=0)  41.7 us
    all_gather x1, blocking collectives, per_device(): left_all = lax.all_gather(left_rows, 'mp', axis=1, tiled=True)  22.6 us
    all_gather x1, waiting for transfers between devices, per_device(): lax.all_gather(right_part.astype(jnp.bfloat16), 'mp', axis=0, tiled=True)  19.9 us
    reshape x1, local copies, waits for them, and re-layouts, per_device(): right_terms.reshape(-1)  9.41 us
    dot_general x1, matrix products, per_device(): jnp.einsum('kmn,kms->kns', compensated, left_rows, preferred_element_type...  8.99 us
  transfers between devices with their start and end apart: 4, of which 4 were waited for; matrix products, arithmetic and copies ran while one was open for 3% of the time, Pallas kernels for 0%

profile of v1, /device:TPU:1, one launch (start us, length us, event | category | flops | bytes accessed | tf_op | source)
XLA Modules:
  0.0 369.6 jit_solution(6850357671872603062)
XLA Ops:
  7.2 0.8 reduce.20
  8.6 3.1 fusion.14
  11.7 50.5 %all-reduce.1 = (f32[8,48,32]{1,2,0:T(8,128)S(1)}, f32[672]{0:T(1024)S(1)}) all-reduce(f32[8,48,32]{1,2,0:T(8,128)S(1)} %fusion.14, f32[672]{0:T(1024)S(1)} %reduce.20), channel_id=1, replica_groups=mesh['replica'=16,'mp'=16] {'replica'}, use_global_device_ids=true, to_apply=%region_0.0 | all-reduce | flops 12960 | bytes 103680 | tf_op jit(solution)/shard_map/psum | solution.py:39
  62.6 9.0 %fusion.12 = f32[8,3072,32]{2,1,0:T(8,128)} fusion(bf16[8,48,32]{1,2,0:T(8,128)(2,1)S(1)} %convolution_convert_fusion, bf16[1,8,48,3072]{3,2,1,0:T(8,128)(2,1)} %param.11, bf16[1,8,48,3072]{3,2,1,0:T(8,128)(2,1)} %param.10), kind=kOutput, calls=%fused_computation.29 | convolution fusion | flops 80216064 | bytes 7888896 | tf_op jit(solution)/shard_map/kmn,kms->kns/dot_general | solution.py:43
  71.6 9.4 %reshape.76 = f32[786432]{0:T(1024)} reshape(f32[8,3072,32]{2,1,0:T(8,128)} %fusion.12) | data formatting | bytes 6291456 | tf_op jit(solution)/shard_map/reshape | solution.py:46
  81.1 0.6 copy-done.8
  81.7 0.6 dynamic-slice.8
  83.0 104.2 %all-reduce.4.cloned.1.call-done = f32[786432]{0:T(1024)} async-done(((f32[786432]{0:T(1024)}), f32[786432]{0:T(1024)}) %all-reduce.4.cloned.1.call-update) | async-done | bytes 3145744
  187.1 1.6 dynamic-slice.9
  188.8 41.7 %all-gather.8.cloned.1.call-done = f32[786432]{0:T(1024)} async-done(((f32[49152]{0:T(1024)}), f32[786432]{0:T(1024)}) %all-gather.8.cloned.1.call-update) | async-done | bytes 3145744 | tf_op jit(solution)/shard_map/all_gather | solution.py:47
  230.5 3.4 reshape.130
  233.9 3.0 reduce_sum.18
  237.3 0.7 bitcast_reduce_fusion
  239.3 0.6 compare_and_fusion
  241.2 22.6 %all_gather.18 = bf16[8,768,32]{2,0,1:T(8,128)(2,1)S(1)} all-gather(bf16[8,48,32]{2,0,1:T(8,128)(2,1)S(1)} %copy.27), channel_id=1, replica_groups=mesh['replica'=16,'mp'=16] {'mp'}, dimensions={1}, use_global_device_ids=true | all-gather | bytes 417792 | tf_op jit(solution)/shard_map/all_gather | solution.py:51
  263.9 19.9 %all-gather.6.cloned.1.call-done = bf16[786432]{0:T(1024)(128)(2,1)} async-done(((bf16[49152]{0:T(1024)(128)(2,1)}), bf16[786432]{0:T(1024)(128)(2,1)}) %all-gather.6.cloned.1.call-update) | async-done | bytes 1572880 | tf_op jit(solution)/shard_map/all_gather | solution.py:48
  283.8 7.8 %reshape.77 = bf16[8,3072,32]{2,1,0:T(8,128)(2,1)} reshape(bf16[786432]{0:T(1024)(128)(2,1)} %all-gather.6.cloned.1.call-done) | data formatting | bytes 3145728 | tf_op jit(solution)/shard_map/reshape | solution.py:48
  291.6 3.0 convolution_add_fusion
  294.6 1.1 fusion.7
  295.8 0.6 multiply_subtract_fusion
  296.4 7.9 %fusion = bf16[1,8,48,3072]{3,2,1,0:T(8,128)(2,1)} fusion(bf16[8,48,32]{1,2,0:T(8,128)(2,1)S(1)} %convolution_convert_fusion, bf16[8,3072,32]{2,1,0:T(8,128)(2,1)} %reshape.77, bf16[1,8,48,3072]{3,2,1,0:T(8,128)(2,1)} %param.11, bf16[1,8,48,3072]{3,2,1,0:T(8,128)(2,1)} %param.10), kind=kOutput, calls=%fused_computation.3 | convolution fusion | flops 83755008 | bytes 8675328 | tf_op jit(solution)/shard_map/kms,kns->kmn/dot_general | solution.py:52
  304.3 51.0 %all-gather.10.cloned.1.call-done = bf16[768,3072]{1,0:T(8,128)(2,1)} async-done(((bf16[48,3072]{1,0:T(8,128)(2,1)}), bf16[768,3072]{1,0:T(8,128)(2,1)}) %all-gather.10.cloned.1.call-update) | async-done | bytes 4718608 | tf_op jit(solution)/shard_map/all_gather | solution.py:68
  355.3 4.4 %gather_fusion = bf16[8,48,3072]{2,1,0:T(8,128)(2,1)} fusion(bf16[16,48,3072]{2,1,0:T(8,128)(2,1)} %bitcast.36, s32[1024]{0:T(1024)S(1)} %pad_clamp_fusion), kind=kCustom, calls=%fused_computation | custom fusion | bytes 4718624 | tf_op jit(solution)/shard_map/jit(_take)/gather | solution.py:69
  359.7 3.4 broadcast_select_fusion
  (30 shorter events, 1.5 us)
Async XLA Ops:
  7.2 1.4 copy-start
  7.2 180.0 %all-reduce.4.cloned.1.call-start = ((), (), s32[]{:S(2)}) async-start(), calls=%async_computation.3 | async-start | bytes 6291456
  8.6 53.6 %copy-start.4 = (f32[8,32,32]{2,1,0:T(8,128)S(1)}, f32[8,32,32]{2,1,0:T(8,128)}, u32[]{:S(2)}) copy-start(f32[8,32,32]{2,1,0:T(8,128)} %param.13) | copy-start | bytes 98308
  81.0 0.7 copy-start.8
  81.1 149.5 %all-gather.8.cloned.1.call-start = ((), (), s32[]{:S(2)}) async-start(), calls=%async_computation.1 | async-start | bytes 3342336 | tf_op jit(solution)/shard_map/all_gather | solution.py:47
  188.8 95.0 %all-gather.6.cloned.1.call-start = ((), (), s32[]{:S(2)}) async-start(), calls=%async_computation | async-start | bytes 1671168 | tf_op jit(solution)/shard_map/all_gather | solution.py:48
  233.9 3.3 copy-start.7
  237.0 118.3 %all-gather.10.cloned.1.call-start = ((), (), s32[]{:S(2)}) async-start(), calls=%async_computation.2 | async-start | bytes 5013504 | tf_op jit(solution)/shard_map/all_gather | solution.py:68
  263.9 27.7 %copy-start.2 = (f32[1,1,48,3072]{3,2,1,0:T(8,128)S(1)}, f32[1,1,48,3072]{3,2,1,0:T(8,128)}, u32[]{:S(2)}) copy-start(f32[1,1,48,3072]{3,2,1,0:T(8,128)} %param.15) | copy-start | bytes 1769476
  291.6 3.0 copy-start.3
  291.6 4.1 %copy-start.5 = (f32[672]{0:T(1024)S(1)}, f32[672]{0:T(1024)}, u32[]{:S(2)}) copy-start(f32[672]{0:T(1024)} %param.19) | copy-start | bytes 8068
  291.6 4.2 %copy-start.6 = (f32[672]{0:T(1024)S(1)}, f32[672]{0:T(1024)}, u32[]{:S(2)}) copy-start(f32[672]{0:T(1024)} %param.18) | copy-start | bytes 8068
  294.6 9.7 %copy-start.1 = (f32[48,3072]{1,0:T(8,128)}, f32[48,3072]{1,0:T(8,128)S(1)}, u32[]{:S(2)}) copy-start(f32[48,3072]{1,0:T(8,128)S(1)} %convolution_add_fusion) | copy-start | bytes 1769476
Sparse Core Ops, SparseCore 0:
  81.2 105.9 all-reduce.3
  189.6 40.9 all-gather.7
  237.1 46.5 all-gather.5
  295.9 59.3 all-gather.9
